TPU v7x, 768 devices: a whole 4x8x12 slice. The times are simulated.
768 devices in a mesh: dp: 48 (over z, y_hi, core), ctx: 16 (over x, y_lo).
Axes of the slice: x: 4, y: 8 (y_hi: 2, y_lo: 4; y = y_hi * 4 + y_lo), z: 12, core: 2. Of those that a mesh axis runs over, the one named last changes fastest.
Arguments:
- queries: bfloat16 [48, 2048, 1152], P('dp', 'ctx')
- key_states: bfloat16 [48, 2048, 1152], P('dp', 'ctx')
- value_states: bfloat16 [48, 2048, 1152], P('dp', 'ctx'), may hold values from -6 to 6
- out_cotangent: bfloat16 [48, 2048, 1024], P('dp', 'ctx'), may hold values from -0.875 to 0.875
- out_weight: bfloat16 [1024, 1152], replicated, may hold values from -3 to 3
- block_clip: int32 [48, 16], P('dp', 'ctx'), may hold values from 0 to 3, never falling along the last dimension, each value on 1 to 13 neighbouring positions
Outputs:
- sublayer_out: bfloat16 [48, 2048, 1024], P('dp', 'ctx')
- query_grad: bfloat16 [48, 2048, 1152], P('dp', 'ctx')
- key_grad: bfloat16 [48, 2048, 1152], P('dp', 'ctx')
- value_grad: bfloat16 [48, 2048, 1152], P('dp', 'ctx')
- weight_grad: float32 [1024, 1152], P('ctx', 'dp')
All inputs are finite; a program needn't handle non-finite values.
Results may differ from a plain program's by a relative error of at most 0.034.
Values may be sent and summed in bfloat16 or wider, within the bound.
A program may use at most 32 MiB of HBM per device.

v0:
```python
import math

import jax
import jax.numpy as jnp
from jax import lax
from jax.sharding import PartitionSpec as P

HEADS = 18
HDIM = 64
BLOCK = 128
WIN = 256


big_negative = -1e30


def passed_along(value, axis, steps):
    count = lax.axis_size(axis)
    first, last = (max(0, -steps), min(count, count - steps))
    return lax.ppermute(value, axis, [(source, source + steps) for source in range(first, last)])


def grouped_heads(matrix, head_count, group):
    rows = matrix.shape[0]
    stacked = matrix.reshape(rows, head_count, -1).transpose(1, 0, 2)
    return stacked.reshape(head_count // group, group, rows, stacked.shape[2])


def merge_groups(grouped):
    heads = grouped.reshape(grouped.shape[0] * grouped.shape[1], grouped.shape[2], grouped.shape[3])
    return heads.transpose(1, 0, 2).reshape(heads.shape[1], -1)


def rounded_back(values):
    return lax.optimization_barrier(values.astype(jnp.bfloat16)).astype(jnp.float32)


def allowed(query_pos, key_pos, query_clip, key_clip, window):
    causal = key_pos[None, :] <= query_pos[:, None]
    inside = query_pos[:, None] - key_pos[None, :] < window
    present = key_pos[None, :] >= 0
    same_clip = query_clip[:, None] == key_clip[None, :]
    return causal & inside & present & same_clip


def forward_block(query_rows, key_rows, value_rows, visible, head_count, scaling):
    group = math.gcd(head_count, 8)

    def forward_one_group(triple):
        query_head, key_head, value_head = triple
        scores = (
            jnp.einsum("hqd,hkd->hqk", query_head, key_head, preferred_element_type=jnp.float32)
            * scaling
        )
        scores = jnp.where(visible[None], scores, big_negative)
        maximum = jnp.max(scores, axis=2, keepdims=True)
        log_total = maximum[:, :, 0] + jnp.log(jnp.sum(jnp.exp(scores - maximum), axis=2))
        weights = jnp.exp(scores - log_total[:, :, None]).astype(jnp.bfloat16)
        mixed = jnp.einsum(
            "hqk,hkd->hqd", weights, value_head, preferred_element_type=jnp.float32
        ).astype(jnp.bfloat16)
        return (mixed, log_total)

    stacked = (
        grouped_heads(query_rows, head_count, group),
        grouped_heads(key_rows, head_count, group),
        grouped_heads(value_rows, head_count, group),
    )
    mixed, log_total = lax.map(forward_one_group, stacked)
    return (merge_groups(mixed), log_total.reshape(head_count, -1))


def backward_block(
    query_rows, key_rows, value_rows, d_rows, log_total, delta, visible, head_count, scaling
):
    group = math.gcd(head_count, 8)

    def backward_one_group(inputs):
        query_head, key_head, value_head, d_head, total_head, delta_head = inputs
        scores = (
            jnp.einsum("hqd,hkd->hqk", query_head, key_head, preferred_element_type=jnp.float32)
            * scaling
        )
        scores = jnp.where(visible[None], scores, big_negative)
        probs = jnp.exp(scores - total_head[:, :, None])
        d_weights = jnp.einsum(
            "hqd,hkd->hqk", d_head, value_head, preferred_element_type=jnp.float32
        )
        d_scores = (probs * (d_weights - delta_head[:, :, None]) * scaling).astype(jnp.bfloat16)
        query_part = jnp.einsum(
            "hqk,hkd->hqd", d_scores, key_head, preferred_element_type=jnp.float32
        )
        key_part = jnp.einsum(
            "hqk,hqd->hkd", d_scores, query_head, preferred_element_type=jnp.float32
        )
        value_part = jnp.einsum(
            "hqk,hqd->hkd", probs.astype(jnp.bfloat16), d_head, preferred_element_type=jnp.float32
        )
        return (query_part, key_part, value_part)

    rows = log_total.shape[1]
    stacked = (
        grouped_heads(query_rows, head_count, group),
        grouped_heads(key_rows, head_count, group),
        grouped_heads(value_rows, head_count, group),
        grouped_heads(d_rows, head_count, group),
        log_total.reshape(head_count // group, group, rows),
        delta.reshape(head_count // group, group, rows),
    )
    query_part, key_part, value_part = lax.map(backward_one_group, stacked)
    return (merge_groups(query_part), merge_groups(key_part), merge_groups(value_part))


def per_device(queries, key_states, value_states, out_cotangent, out_weight, block_clip):
    row_count = queries.shape[1]
    width = queries.shape[2]
    head_count = HEADS
    scaling = 1.0 / math.sqrt(HDIM)
    window = WIN
    query_own = queries[0]
    key_own = key_states[0]
    value_own = value_states[0]
    cotangent_own = out_cotangent[0]
    clip_steps = jnp.repeat(block_clip[0], BLOCK)
    reach = min(row_count, window)
    hop_count = min(window // reach, lax.axis_size("ctx") - 1)
    anchor = lax.axis_index("ctx") * row_count
    tail_rows = (key_own, value_own, clip_steps)
    received = []
    for hop_index in range(1, hop_count + 1):
        received.append(passed_along((tail_rows[0], tail_rows[1], tail_rows[2]), "ctx", hop_index))
    front_rows = window - hop_count * reach
    earlier = list(reversed(received))
    key_cat = jnp.concatenate(
        [jnp.zeros((front_rows, width), jnp.bfloat16)]
        + [piece[0] for piece in earlier]
        + [key_own],
        axis=0,
    )
    value_cat = jnp.concatenate(
        [jnp.zeros((front_rows, width), jnp.bfloat16)]
        + [piece[1] for piece in earlier]
        + [value_own],
        axis=0,
    )
    clip_cat = jnp.concatenate(
        [jnp.full((front_rows,), -1, jnp.int32)] + [piece[2] for piece in earlier] + [clip_steps],
        axis=0,
    )
    key_positions = anchor - window + jnp.arange(window + row_count, dtype=jnp.int32)
    block_rows = min(row_count, 512)
    block_start = 0
    query_pos = anchor + block_start + jnp.arange(block_rows, dtype=jnp.int32)
    visible = allowed(query_pos, key_positions, clip_steps, clip_cat, window)
    masks = [visible]
    mixed, log_total = forward_block(query_own, key_cat, value_cat, visible, head_count, scaling)
    sublayer_out = lax.dot_general(
        mixed, out_weight, (((1,), (1,)), ((), ())), preferred_element_type=jnp.float32
    ).astype(jnp.bfloat16)
    d_attended = jnp.dot(cotangent_own, out_weight, preferred_element_type=jnp.float32).astype(
        jnp.bfloat16
    )
    delta = jnp.sum(
        (d_attended.astype(jnp.float32) * mixed.astype(jnp.float32)).reshape(
            row_count, head_count, -1
        ),
        axis=2,
    ).T
    query_parts = []
    key_acc = jnp.zeros((window + row_count, width), jnp.float32)
    value_acc = jnp.zeros((window + row_count, width), jnp.float32)
    for number, block_start in enumerate(range(0, row_count, block_rows)):
        stop = block_start + block_rows
        query_part, key_part, value_part = backward_block(
            query_own,
            key_cat,
            value_cat,
            d_attended,
            log_total,
            delta,
            masks[number],
            head_count,
            scaling,
        )
        query_parts.append(query_part.astype(jnp.bfloat16))
        key_acc = key_acc.at[block_start : stop + window].add(key_part)
        value_acc = value_acc.at[block_start : stop + window].add(value_part)
    query_grad = query_parts[0]
    key_total = rounded_back(key_acc[window:])
    value_total = rounded_back(value_acc[window:])
    key_tail = jnp.zeros((reach, width), jnp.float32)
    value_tail = jnp.zeros((reach, width), jnp.float32)
    for hop_index in range(1, hop_count + 1):
        lower = window - hop_index * reach
        outgoing = (
            key_acc[lower : lower + reach].astype(jnp.bfloat16),
            value_acc[lower : lower + reach].astype(jnp.bfloat16),
        )
        incoming = passed_along((outgoing[0], outgoing[1]), "ctx", -hop_index)
        key_tail = key_tail + incoming[0].astype(jnp.float32)
        value_tail = value_tail + incoming[1].astype(jnp.float32)
    key_total = key_total.at[row_count - reach :].add(key_tail)
    value_total = value_total.at[row_count - reach :].add(value_tail)
    piece = cotangent_own
    sequence_grad = lax.psum_scatter(
        lax.dot_general(
            piece, mixed, (((0,), (0,)), ((), ())), preferred_element_type=jnp.float32
        ).astype(jnp.bfloat16),
        "ctx",
        scatter_dimension=0,
        tiled=True,
    ).astype(jnp.float32)
    weight_grad = lax.psum_scatter(sequence_grad, "dp", scatter_dimension=1, tiled=True)
    return (
        sublayer_out[None],
        query_grad[None],
        key_total.astype(jnp.bfloat16)[None],
        value_total.astype(jnp.bfloat16)[None],
        weight_grad,
    )


def solution(mesh):
    return jax.shard_map(
        per_device,
        mesh=mesh,
        in_specs=(
            P("dp", "ctx", None),
            P("dp", "ctx", None),
            P("dp", "ctx", None),
            P("dp", "ctx", None),
            P(),
            P("dp", "ctx"),
        ),
        out_specs=(
            P("dp", "ctx", None),
            P("dp", "ctx", None),
            P("dp", "ctx", None),
            P("dp", "ctx", None),
            P("ctx", "dp"),
        ),
        check_vma=False,
    )
```

profile of v0, /device:TPU:6, one launch (start us, length us, event | category | flops | bytes accessed | tf_op | source)
XLA Modules:
  0.0 420.4 jit_solution(17277968071175240682)
XLA Ops:
  8.5 4.5 %collective-permute-start.4 = (bf16[128,1152]{0,1:T(8,128)(2,1)S(1)}, bf16[128,1152]{0,1:T(8,128)(2,1)}, u32[]{:S(2)}, u32[]{:S(2)}) collective-permute-start(bf16[128,1152]{0,1:T(8,128)(2,1)S(1)} %bitcast.174), channel_id=1, source_target_pairs={{0,2},{1,3},{2,4},{3,5},{4,6},{5,7},{6,8},{7,9},{8,10},{9,11},{10,... | collective-permute-start | bytes 884744 | tf_op jit(solution)/shard_map/ppermute | solution.py:20
  13.0 3.5 collective-permute-start.5
  17.7 1.9 collective-permute-start.2
  19.6 1.9 collective-permute-start.3
  22.2 1.9 collective-permute-start
  24.2 28.4 %collective-permute-done = s32[128]{0:T(128)S(1)} collective-permute-done((s32[128]{0:T(128)S(1)}, s32[128]{0:T(128)S(1)}, u32[]{:S(2)}, u32[]{:S(2)}) %collective-permute-start) | collective-permute-done | bytes 544 | tf_op jit(solution)/shard_map/ppermute | solution.py:20
  53.2 1.9 collective-permute-start.1
  55.2 1.8 copy.34
  57.0 4.3 %collective-permute-done.1 = s32[128]{0:T(128)} collective-permute-done((s32[128]{0:T(128)S(1)}, s32[128]{0:T(128)}, u32[]{:S(2)}, u32[]{:S(2)}) %collective-permute-start.1) | collective-permute-done | bytes 544 | tf_op jit(solution)/shard_map/ppermute | solution.py:20
  62.0 2.1 pad_maximum_fusion.1
  66.1 29.1 %while.36 = (s32[]{:T(128)}, bf16[9,2,128,64]{2,3,1,0:T(8,128)(2,1)S(1)}, f32[9,2,128]{2,1,0:T(2,128)}, bf16[9,2,128,64]{2,3,1,0:T(8,128)(2,1)}, bf16[9,2,384,64...) while((s32[]{:T(128)}, ...), condition=%wide.region_3.4_spmd.clone, body=%wide.region_0.3_spmd.clone.sunk | while | flops 26164992 | bytes 1553773 | solution.py:69
  96.1 3.2 fusion.53
  100.7 2.1 copy.41
  107.7 4.3 %copy.45 = bf16[1024,1152]{1,0:T(8,128)(2,1)} copy(bf16[1024,1152]{0,1:T(8,128)(2,1)} %fusion.53) | data formatting | bytes 4718592
  112.1 63.1 %while.37 = (s32[]{:T(128)}, bf16[9,2,128,64]{2,3,1,0:T(8,128)(2,1)}, bf16[9,2,384,64]{2,3,1,0:T(8,128)(2,1)}, bf16[9,2,384,64]{2,3,1,0:T(8,128)(2,1)}, bf16[9,2...) while((s32[]{:T(128)}, ...), condition=%wide.region_6.7_spmd.clone, body=%wide.region_5.6_spmd.clone.sunk | while | flops 63995904 | bytes 2766737 | solution.py:110
  175.2 2.1 fusion.60
  177.3 2.3 collective-permute-start.8
  179.6 1.9 collective-permute-start.9
  182.6 6.1 %collective-permute-start.6 = (bf16[128,1152]{0,1:T(8,128)(2,1)}, bf16[128,1152]{0,1:T(8,128)(2,1)}, u32[]{:S(2)}, u32[]{:S(2)}) collective-permute-start(bf16[128,1152]{0,1:T(8,128)(2,1)} %bitcast.39), channel_id=1, source_target_pairs={{1,0},{2,1},{3,2},{4,3},{5,4},{6,5},{7,6},{8,7},{9,8},{10,9},{11,1... | collective-permute-start | bytes 884744 | tf_op jit(solution)/shard_map/ppermute | solution.py:20
  188.7 1.9 collective-permute-start.7
  190.6 1.8 copy.42
  194.9 16.8 %collective-permute-done.9 = bf16[128,1152]{0,1:T(8,128)(2,1)} collective-permute-done((bf16[128,1152]{0,1:T(8,128)(2,1)}, bf16[128,1152]{0,1:T(8,128)(2,1)}, u32[]{:S(2)}, u32[]{:S(2)}) %collective-permute-start.9) | collective-permute-done | bytes 294944 | tf_op jit(solution)/shard_map/ppermute | solution.py:20
  213.8 18.3 %reduce-scatter.7.cloned.1.call-done = bf16[64,1152]{1,0:T(8,128)(2,1)} async-done(((bf16[1024,1152]{1,0:T(8,128)(2,1)}), bf16[64,1152]{1,0:T(8,128)(2,1)}) %reduce-scatter.7.cloned.1.call-update) | async-done | bytes 147472
  237.7 175.8 %reduce-scatter.9.cloned.1.call-done = f32[64,24]{0,1:T(8,128)} async-done(((f32[64,1152]{0,1:T(8,128)}), f32[64,24]{0,1:T(8,128)}) %reduce-scatter.9.cloned.1.call-update) | async-done | bytes 6160
  (161 shorter events, 115.8 us)
Async XLA Ops:
  7.2 92.1 %copy-start = (bf16[1024,1152]{1,0:T(8,128)(2,1)S(1)}, bf16[1024,1152]{1,0:T(8,128)(2,1)}, u32[]{:S(2)}) copy-start(bf16[1024,1152]{1,0:T(8,128)(2,1)} %param.30) | copy-start | bytes 7077892
  7.2 225.0 %reduce-scatter.7.cloned.1.call-start = ((), (), s32[]{:S(2)}) async-start(), calls=%async_computation.2 | async-start | bytes 2506752
  8.5 53.4 %collective-permute-start.4 = (bf16[128,1152]{0,1:T(8,128)(2,1)S(1)}, bf16[128,1152]{0,1:T(8,128)(2,1)}, u32[]{:S(2)}, u32[]{:S(2)}) collective-permute-start(bf16[128,1152]{0,1:T(8,128)(2,1)S(1)} %bitcast.174), channel_id=1, source_target_pairs={{0,2},{1,3},{2,4},{3,5},{4,6},{5,7},{6,8},{7,9},{8,10},{9,11},{10,... | collective-permute-start | bytes 884744 | tf_op jit(solution)/shard_map/ppermute | solution.py:20
  13.0 48.9 %collective-permute-start.5 = (bf16[128,1152]{0,1:T(8,128)(2,1)S(1)}, bf16[128,1152]{0,1:T(8,128)(2,1)}, u32[]{:S(2)}, u32[]{:S(2)}) collective-permute-start(bf16[128,1152]{0,1:T(8,128)(2,1)S(1)} %bitcast.175), channel_id=1, source_target_pairs={{0,1},{1,2},{2,3},{3,4},{4,5},{5,6},{6,7},{7,8},{8,9},{9,10},{10,1... | collective-permute-start | bytes 884744 | tf_op jit(solution)/shard_map/ppermute | solution.py:20
  17.7 46.4 %copy-start.1 = (bf16[1,128,1152]{1,2,0:T(8,128)(2,1)}, bf16[1,128,1152]{1,2,0:T(8,128)(2,1)S(1)}, u32[]{:S(2)}) copy-start(bf16[1,128,1152]{1,2,0:T(8,128)(2,1)S(1)} %copy.35) | copy-start | bytes 884740
  17.7 46.4 %collective-permute-start.2 = (bf16[128,1152]{0,1:T(8,128)(2,1)S(1)}, bf16[128,1152]{0,1:T(8,128)(2,1)S(1)}, u32[]{:S(2)}, u32[]{:S(2)}) collective-permute-start(bf16[128,1152]{0,1:T(8,128)(2,1)S(1)} %bitcast.171), channel_id=1, source_target_pairs={{0,2},{1,3},{2,4},{3,5},{4,6},{5,7},{6,8},{7,9},{8,10},{9,11},{10,... | collective-permute-start | bytes 884744 | tf_op jit(solution)/shard_map/ppermute | solution.py:20
  19.6 44.4 %collective-permute-start.3 = (bf16[128,1152]{0,1:T(8,128)(2,1)S(1)}, bf16[128,1152]{0,1:T(8,128)(2,1)}, u32[]{:S(2)}, u32[]{:S(2)}) collective-permute-start(bf16[128,1152]{0,1:T(8,128)(2,1)S(1)} %bitcast.172), channel_id=1, source_target_pairs={{0,1},{1,2},{2,3},{3,4},{4,5},{5,6},{6,7},{7,8},{8,9},{9,10},{10,1... | collective-permute-start | bytes 884744 | tf_op jit(solution)/shard_map/ppermute | solution.py:20
  22.2 39.0 %copy-start.6 = (s32[128]{0:T(128)}, s32[128]{0:T(128)S(1)}, u32[]{:S(2)}) copy-start(s32[128]{0:T(128)S(1)} %reshape.235) | copy-start | bytes 1540
  22.2 30.4 %collective-permute-start = (s32[128]{0:T(128)S(1)}, s32[128]{0:T(128)S(1)}, u32[]{:S(2)}, u32[]{:S(2)}) collective-permute-start(s32[128]{0:T(128)S(1)} %reshape.235), channel_id=1, source_target_pairs={{0,2},{1,3},{2,4},{3,5},{4,6},{5,7},{6,8},{7,9},{8,10},{9,11},{10,... | collective-permute-start | bytes 1544 | tf_op jit(solution)/shard_map/ppermute | solution.py:20
  52.7 0.5 copy-start.7
  53.2 8.1 %collective-permute-start.1 = (s32[128]{0:T(128)S(1)}, s32[128]{0:T(128)}, u32[]{:S(2)}, u32[]{:S(2)}) collective-permute-start(s32[128]{0:T(128)S(1)} %reshape.235), channel_id=1, source_target_pairs={{0,1},{1,2},{2,3},{3,4},{4,5},{5,6},{6,7},{7,8},{8,9},{9,10},{10,1... | collective-permute-start | bytes 1544 | tf_op jit(solution)/shard_map/ppermute | solution.py:20
  64.1 0.7 copy-start.5
  96.1 3.2 copy-start.2
  96.1 3.2 copy-start.3
  112.1 301.4 %reduce-scatter.9.cloned.1.call-start = ((), (), s32[]{:S(2)}) async-start(), calls=%async_computation.3 | async-start | bytes 602112
  175.2 6.4 %copy-start.4 = (bf16[9,2,384,64]{2,3,1,0:T(8,128)(2,1)S(1)}, bf16[9,2,384,64]{2,3,1,0:T(8,128)(2,1)}, u32[]{:S(2)}) copy-start(bf16[9,2,384,64]{2,3,1,0:T(8,128)(2,1)} %get-tuple-element.185) | copy-start | bytes 2654212
  177.3 17.6 %collective-permute-start.8 = (bf16[128,1152]{0,1:T(8,128)(2,1)}, bf16[128,1152]{0,1:T(8,128)(2,1)}, u32[]{:S(2)}, u32[]{:S(2)}) collective-permute-start(bf16[128,1152]{0,1:T(8,128)(2,1)} %bitcast.46), channel_id=1, source_target_pairs={{1,0},{2,1},{3,2},{4,3},{5,4},{6,5},{7,6},{8,7},{9,8},{10,9},{11,1... | collective-permute-start | bytes 884744 | tf_op jit(solution)/shard_map/ppermute | solution.py:20
  179.6 32.1 %collective-permute-start.9 = (bf16[128,1152]{0,1:T(8,128)(2,1)}, bf16[128,1152]{0,1:T(8,128)(2,1)}, u32[]{:S(2)}, u32[]{:S(2)}) collective-permute-start(bf16[128,1152]{0,1:T(8,128)(2,1)} %bitcast.47), channel_id=1, source_target_pairs={{2,0},{3,1},{4,2},{5,3},{6,4},{7,5},{8,6},{9,7},{10,8},{11,9},{12,... | collective-permute-start | bytes 884744 | tf_op jit(solution)/shard_map/ppermute | solution.py:20
  182.6 51.6 %collective-permute-start.6 = (bf16[128,1152]{0,1:T(8,128)(2,1)}, bf16[128,1152]{0,1:T(8,128)(2,1)}, u32[]{:S(2)}, u32[]{:S(2)}) collective-permute-start(bf16[128,1152]{0,1:T(8,128)(2,1)} %bitcast.39), channel_id=1, source_target_pairs={{1,0},{2,1},{3,2},{4,3},{5,4},{6,5},{7,6},{8,7},{9,8},{10,9},{11,1... | collective-permute-start | bytes 884744 | tf_op jit(solution)/shard_map/ppermute | solution.py:20
  188.7 47.0 %collective-permute-start.7 = (bf16[128,1152]{0,1:T(8,128)(2,1)S(1)}, bf16[128,1152]{0,1:T(8,128)(2,1)}, u32[]{:S(2)}, u32[]{:S(2)}) collective-permute-start(bf16[128,1152]{0,1:T(8,128)(2,1)S(1)} %bitcast.182), channel_id=1, source_target_pairs={{2,0},{3,1},{4,2},{5,3},{6,4},{7,5},{8,6},{9,7},{10,8},{11,9},{12,... | collective-permute-start | bytes 884744 | tf_op jit(solution)/shard_map/ppermute | solution.py:20
Sparse Core Ops, SparseCore 0:
  112.2 119.9 reduce-scatter.6
  237.9 175.5 reduce-scatter.8
where the time goes:
time: 424 us; the launch traced here: 420 us
  waiting for transfers between devices  246 us (58%)
  matrix products  82.3 us (19%)
  local copies, waits for them, and re-layouts  30.1 us (7%)
  starting transfers between devices  28 us (7%)
  other arithmetic  18.4 us (4%)
  between operations  14.9 us (4%)
    unnamed x4, waiting for transfers between devices  194 us
    ppermute x10, waiting for transfers between devices, passed_along(): lax.ppermute(value, axis, [(source, source + steps) for source in range(f...  51.9 us
    ppermute x10, starting transfers between devices, passed_along(): lax.ppermute(value, axis, [(source, source + steps) for source in range(f...  27.9 us
    unnamed x24, local copies, waits for them, and re-layouts  14.7 us
    dot_general x9, matrix products, backward_one_group(): jnp.einsum('hqk,hqd->hkd', d_scores, query_head, preferred_element_type=j...  14.2 us
    dot_general x9, matrix products, backward_one_group(): jnp.einsum('hqk,hqd->hkd', probs.astype(jnp.bfloat16), d_head, preferred_...  14.1 us
    dot_general x9, matrix products, backward_one_group(): jnp.einsum('hqd,hkd->hqk', d_head, value_head, preferred_element_type=jnp...  10.6 us
    dot_general x9, matrix products, forward_one_group(): jnp.einsum('hqk,hkd->hqd', weights, value_head, preferred_element_type=jn...  10.6 us
  transfers between devices with their start and end apart: 12, of which 7 were waited for; matrix products, arithmetic and copies ran while one was open for 19% of the time, Pallas kernels for 0%

commit v1 on v0

v1 whole, which is shorter than its diff:
```python
import math

import jax
import jax.numpy as jnp
from jax import lax
from jax.experimental import pallas as pl
from jax.experimental.pallas import tpu as pltpu
from jax.sharding import PartitionSpec as P

HDIM = 64
BLOCK = 128
WIN = 256
GROUPS = 3
PAIR = 2 * HDIM

NZ, NYH, NC = 12, 2, 2
NX, NYL = 4, 4

BF16 = jnp.bfloat16
F32 = jnp.float32
MESH = pl.DeviceIdType.MESH


def dot_nn(a, b):
    return lax.dot_general(a, b, (((1,), (0,)), ((), ())), preferred_element_type=F32)


def dot_nt(a, b):
    return lax.dot_general(a, b, (((1,), (1,)), ((), ())), preferred_element_type=F32)


def dot_tn(a, b):
    return lax.dot_general(a, b, (((0,), (0,)), ((), ())), preferred_element_type=F32)


def kernel(
    clip_ref, q_ref, k_ref, v_ref, cot_ref, w_ref,
    out_ref, dq_ref, dk_ref, dv_ref, wg_ref,
    kcat, vcat, clips, bias, da_buf, att_buf,
    own_k, own_v, near_k, near_v, far_k, far_v, sum_k, sum_v,
    in_far_k, in_far_v, in_near_k, in_near_v,
    g_buf, a_in, b_buf, b_in, z_buf, z_in, y_buf, y_in, t_buf,
    clip_sem, halo_sem, back_sem, a_sem, b_sem, z_send, z_recv, y_send, y_recv,
):
    dp, ctx = lax.axis_index("dp"), lax.axis_index("ctx")
    n_ctx = NX * NYL
    core = lax.rem(dp, NC)
    yh = lax.rem(dp // NC, NYH)
    z = dp // (NC * NYH)
    x, yl = ctx // NYL, lax.rem(ctx, NYL)
    here = yh * NYL + yl
    gw = q_ref.shape[1] // GROUPS
    dout = cot_ref.shape[1]
    dx = dout // NX
    zg = NZ // GROUPS
    rows = gw // (zg * NYH * NC)
    yw = dx // NYL
    yc = max(yw, 128)

    right = (dp, lax.rem(ctx + 1, n_ctx))
    left = (dp, lax.rem(ctx + n_ctx - 1, n_ctx))
    sibling = (dp - core + (NC - 1 - core), ctx)

    def at_x(d):
        return (dp, lax.rem(x + d, NX) * NYL + yl)

    def at_z(zz):
        return ((zz * NYH + yh) * NC + core, ctx)

    def at_y(k):
        return ((z * NYH + k // NYL) * NC + core, x * NYL + lax.rem(k, NYL))

    barrier = pltpu.get_barrier_semaphore()

    def hello(device):
        pl.semaphore_signal(barrier, inc=1, device_id=device, device_id_type=MESH)

    hello(right)
    hello(left)
    hello(sibling)
    for d in range(1, NX):
        hello(at_x(d))
    if NZ > 1:
        @pl.loop(1, NZ)
        def _(d):
            hello(at_z(lax.rem(z + d, NZ)))
    if NYH * NYL > 1:
        @pl.loop(1, NYH * NYL)
        def _(d):
            hello(at_y(lax.rem(here + d, NYH * NYL)))

    clips[2] = jnp.full((8, 128), clip_ref[0, 0], jnp.int32)
    for g in range(GROUPS):
        kcat[g, 2 * BLOCK :, :] = k_ref[:, g * gw : (g + 1) * gw]
        vcat[g, 2 * BLOCK :, :] = v_ref[:, g * gw : (g + 1) * gw]
    pl.semaphore_wait(barrier, 3 + (NX - 1) + (NZ - 1) + (NYH * NYL - 1))

    sends = []

    def remote(src, dst, send_sem, recv_sem, device):
        return pltpu.make_async_remote_copy(
            src_ref=src, dst_ref=dst, send_sem=send_sem, recv_sem=recv_sem,
            device_id=device, device_id_type=MESH,
        )

    def start(copy):
        copy.start()
        sends.append(copy)
        return copy

    def halo(g, hop):
        low = (1 - hop) * BLOCK
        part = []
        for number, cat in enumerate((kcat, vcat)):
            part.append(
                remote(
                    cat.at[g, pl.ds(low + BLOCK, BLOCK), :],
                    cat.at[g, pl.ds(low, BLOCK), :],
                    halo_sem.at[0, hop, g, number],
                    halo_sem.at[1, hop, g, number],
                    right,
                )
            )
        return part

    def clip_hop(hop):
        return remote(
            clips.at[2 - hop], clips.at[1 - hop], clip_sem.at[0, hop], clip_sem.at[1, hop], right
        )

    first = [clip_hop(0)]
    hops = [[halo(g, 0) for g in range(GROUPS)], [halo(g, 1) for g in range(GROUPS)]]
    start(first[0])
    for g in range(GROUPS):
        for copy in hops[0][g]:
            start(copy)

    def d_attended(g):
        cols = slice(g * gw, (g + 1) * gw)
        da_buf[:, cols] = dot_nn(cot_ref[...], w_ref[:, cols]).astype(BF16)

    first[0].wait_recv()
    second = start(clip_hop(1))
    for g in range(GROUPS):
        d_attended(g)
        for number in range(2):
            hops[0][g][number].wait_recv()
            start(hops[1][g][number])
    second.wait_recv()

    row = lax.broadcasted_iota(jnp.int32, (BLOCK, BLOCK), 0)
    col = lax.broadcasted_iota(jnp.int32, (BLOCK, BLOCK), 1)
    own_clip = clips[2, 0:1, :]
    for part in range(3):
        shown = clips[part, 0:1, :] == own_clip
        shown = jnp.broadcast_to(shown, (BLOCK, BLOCK))
        if part == 0:
            shown = shown & (col > row)
        if part == 2:
            shown = shown & (col <= row)
        shown = shown & (col + (ctx + part - 2) * BLOCK >= 0)
        term = jnp.where(shown, 0.0, -1e30).astype(F32)
        cols = slice(part * BLOCK, (part + 1) * BLOCK)
        bias[0:BLOCK, cols] = term
        bias[BLOCK:, cols] = term

    scaling = 1.0 / math.sqrt(HDIM)
    lane = lax.broadcasted_iota(jnp.int32, (BLOCK, PAIR), 1)
    low_head = lane < HDIM

    def stacked(value):
        return jnp.concatenate(
            [jnp.where(low_head, value, 0.0), jnp.where(low_head, 0.0, value)], axis=0
        )

    def picked(value):
        return jnp.where(low_head, value[:BLOCK], value[BLOCK:])

    def attention(g):
        @pl.loop(0, gw // PAIR)
        def _(p):
            lanes = pl.ds(pl.multiple_of(p * PAIR, PAIR), PAIR)
            whole = pl.ds(pl.multiple_of(g * gw + p * PAIR, PAIR), PAIR)
            q2 = stacked(q_ref[:, whole].astype(F32) * scaling).astype(BF16)
            da_f32 = stacked(da_buf[:, whole].astype(F32))
            da2 = da_f32.astype(BF16)
            keys = kcat[g, :, lanes]
            values = vcat[g, :, lanes]
            scores = dot_nt(q2, keys) + bias[...]
            top = jnp.max(scores, axis=1, keepdims=True)
            powers = jnp.exp(scores - top)
            probs = powers * (1.0 / jnp.sum(powers, axis=1, keepdims=True))
            weights = probs.astype(BF16)
            attended = picked(dot_nn(weights, values)).astype(BF16)
            att_buf[:, whole] = attended
            att_f32 = attended.astype(F32)
            delta = jnp.sum(da_f32 * jnp.concatenate([att_f32, att_f32], axis=0), axis=1, keepdims=True)
            d_weights = dot_nt(da2, values)
            d_scores = (probs * (d_weights - delta)).astype(BF16)
            dq_ref[:, whole] = (picked(dot_nn(d_scores, keys)) * scaling).astype(BF16)
            key_part = dot_tn(d_scores, q2)
            value_part = dot_tn(weights, da2)
            for part, far, near, own in (
                (key_part, far_k, near_k, own_k),
                (value_part, far_v, near_v, own_v),
            ):
                far[g, :, lanes] = part[0:BLOCK].astype(BF16)
                near[g, :, lanes] = part[BLOCK : 2 * BLOCK]
                own[g, :, lanes] = part[2 * BLOCK :]

    def far_back(g):
        return [
            remote(far.at[g], into.at[g], back_sem.at[0, 0, g, n], back_sem.at[1, 0, g, n], left)
            for n, (far, into) in enumerate(((far_k, in_far_k), (far_v, in_far_v)))
        ]

    def near_back(g):
        return [
            remote(mid.at[g], into.at[g], back_sem.at[0, 1, g, n], back_sem.at[1, 1, g, n], left)
            for n, (mid, into) in enumerate(((sum_k, in_near_k), (sum_v, in_near_v)))
        ]

    far_copies = [far_back(g) for g in range(GROUPS)]
    near_copies = [near_back(g) for g in range(GROUPS)]

    def relay_back(g):
        for n, (near, into, mid) in enumerate(((near_k, in_far_k, sum_k), (near_v, in_far_v, sum_v))):
            far_copies[g][n].wait_recv()
            mid[g] = (near[g] + into[g].astype(F32)).astype(BF16)
            start(near_copies[g][n])

    def finish_back(g):
        cols = slice(g * gw, (g + 1) * gw)
        for n, (own, into, result) in enumerate(((own_k, in_near_k, dk_ref), (own_v, in_near_v, dv_ref))):
            near_copies[g][n].wait_recv()
            result[:, cols] = (own[g] + into[g].astype(F32)).astype(BF16)

    half = gw // NC

    def a_copy(g):
        return remote(
            g_buf.at[NC - 1 - core, g], a_in.at[g], a_sem.at[0, g], a_sem.at[1, g], sibling
        )

    a_copies = [a_copy(g) for g in range(GROUPS)]

    def weight_terms(g):
        for part in range(NX):
            terms = dot_tn(
                att_buf[:, g * gw : (g + 1) * gw], cot_ref[:, part * dx : (part + 1) * dx]
            ).reshape(zg * NYH, NC, rows, dx)
            for number in range(NC):
                g_buf[number, g, part] = terms[:, number].reshape(half, dx).astype(BF16)
        start(a_copies[g])

    def b_copy(g, d):
        return remote(
            b_buf.at[g, lax.rem(x + d, NX)], b_in.at[g, d - 1],
            b_sem.at[0, g, d - 1], b_sem.at[1, g, d - 1], at_x(d),
        )

    b_copies = [[b_copy(g, d) for d in range(1, NX)] for g in range(GROUPS)]

    def after_core(g):
        a_copies[g].wait_recv()
        for part in range(NX):
            b_buf[g, part] = (g_buf[core, g, part].astype(F32) + a_in[g, part].astype(F32)).astype(BF16)
        for copy in b_copies[g]:
            start(copy)

    def z_copy(g, j):
        return remote(
            z_buf.at[g, j], z_in.at[z], z_send.at[g * zg + j], z_recv.at[z], at_z(g * zg + j)
        )

    def after_x(g):
        total = b_buf[g, x].astype(F32)
        for d in range(1, NX):
            b_copies[g][d - 1].wait_recv()
            total = total + b_in[g, d - 1].astype(F32)
        z_buf[g] = total.reshape(zg, half // zg, dx).astype(BF16)
        for j in range(zg):
            @pl.when(z != g * zg + j)
            def _():
                z_copy(g, j).start()

            @pl.when(z == g * zg + j)
            def _():
                z_in[z] = z_buf[g, j]

    def y_copy(k):
        return remote(
            y_buf.at[pl.ds((k // NYL) * rows, rows), pl.ds(((k % NYL) * yw) // yc * yc, yc)],
            y_in.at[here], y_send.at[k], y_recv.at[here], at_y(k),
        )

    def after_z():
        @pl.loop(0, NZ)
        def _(s):
            @pl.when(s != z)
            def _():
                remote(z_buf.at[0, 0], z_in.at[s], z_send.at[s], z_recv.at[s], at_z(s)).wait_recv()
        total = z_in[0].astype(F32)
        for s in range(1, NZ):
            total = total + z_in[s].astype(F32)
        y_buf[...] = total
        for k in range(NYH * NYL):
            @pl.when(k != here)
            def _():
                y_copy(k).start()

            @pl.when(k == here)
            def _():
                low = ((k % NYL) * yw) // yc * yc
                y_in[here] = y_buf[(k // NYL) * rows : (k // NYL + 1) * rows, low : low + yc]

    def after_y():
        @pl.loop(0, NYH * NYL)
        def _(s):
            @pl.when(s != here)
            def _():
                remote(
                    y_buf.at[pl.ds(0, rows), pl.ds(0, yc)], y_in.at[s], y_send.at[s], y_recv.at[s], at_y(s)
                ).wait_recv()
        total = y_in[0]
        for s in range(1, NYH * NYL):
            total = total + y_in[s]
        t_buf[...] = total.T
        offset = lax.rem(yl * yw, yc)
        wg_ref[...] = t_buf[pl.ds(pl.multiple_of(offset, 8), yw), :]

    def project(part):
        piece = slice(part * dx, (part + 1) * dx)
        out_ref[:, piece] = dot_nt(att_buf[...], w_ref[piece, :]).astype(BF16)

    for g in range(GROUPS):
        for copy in hops[1][g]:
            copy.wait_recv()
        attention(g)
        for copy in far_copies[g]:
            start(copy)
        weight_terms(g)
        if g >= 1:
            relay_back(g - 1)
            after_core(g - 1)
        if g >= 2:
            after_x(g - 2)
    after_core(GROUPS - 1)
    relay_back(GROUPS - 1)
    after_x(GROUPS - 2)
    for part in range(NX):
        project(part)
    after_x(GROUPS - 1)
    for g in range(GROUPS - 1):
        finish_back(g)
    after_z()
    finish_back(GROUPS - 1)
    after_y()

    for copy in sends:
        copy.wait_send()

    @pl.loop(0, NZ)
    def _(s):
        @pl.when(s != z)
        def _():
            remote(z_buf.at[0, 0], z_in.at[s], z_send.at[s], z_recv.at[s], at_z(s)).wait_send()

    @pl.loop(0, NYH * NYL)
    def _(s):
        @pl.when(s != here)
        def _():
            remote(
                y_buf.at[pl.ds(0, rows), pl.ds(0, yc)], y_in.at[s], y_send.at[s], y_recv.at[s], at_y(s)
            ).wait_send()


def per_device(queries, key_states, value_states, out_cotangent, out_weight, block_clip):
    steps, width = queries.shape[1:]
    dout = out_cotangent.shape[2]
    gw = width // GROUPS
    dx = dout // NX
    zg = NZ // GROUPS
    rows = gw // (zg * NYH * NC)
    half = gw // NC
    yw = dx // NYL
    yc = max(yw, 128)
    ny = NYH * NYL
    shape = jax.ShapeDtypeStruct
    vmem = pltpu.VMEM
    dma = pltpu.SemaphoreType.DMA
    group_bf16 = vmem((GROUPS, BLOCK, gw), BF16)
    group_f32 = vmem((GROUPS, BLOCK, gw), F32)
    out, dq, dk, dv, wg = pl.pallas_call(
        kernel,
        out_shape=(
            shape((steps, dout), BF16),
            shape((steps, width), BF16),
            shape((steps, width), BF16),
            shape((steps, width), BF16),
            shape((yw, rows), F32),
        ),
        in_specs=[pl.BlockSpec(memory_space=pltpu.SMEM)] + [pl.BlockSpec(memory_space=vmem)] * 5,
        out_specs=tuple([pl.BlockSpec(memory_space=vmem)] * 5),
        scratch_shapes=[
            vmem((GROUPS, WIN + BLOCK, gw), BF16),
            vmem((GROUPS, WIN + BLOCK, gw), BF16),
            vmem((3, 8, 128), jnp.int32),
            vmem((2 * BLOCK, WIN + BLOCK), F32),
            vmem((steps, width), BF16),
            vmem((steps, width), BF16),
            group_f32, group_f32, group_f32, group_f32,
            group_bf16, group_bf16, group_bf16, group_bf16,
            group_bf16, group_bf16, group_bf16, group_bf16,
            vmem((NC, GROUPS, NX, half, dx), BF16),
            vmem((GROUPS, NX, half, dx), BF16),
            vmem((GROUPS, NX, half, dx), BF16),
            vmem((GROUPS, max(NX - 1, 1), half, dx), BF16),
            vmem((GROUPS, zg, half // zg, dx), BF16),
            vmem((NZ, half // zg, dx), BF16),
            vmem((half // zg, dx), F32),
            vmem((ny, rows, yc), F32),
            vmem((yc, rows), F32),
            dma((2, 2)),
            dma((2, 2, GROUPS, 2)),
            dma((2, 2, GROUPS, 2)),
            dma((2, GROUPS)),
            dma((2, GROUPS, max(NX - 1, 1))),
            dma((NZ,)),
            dma((NZ,)),
            dma((ny,)),
            dma((ny,)),
        ],
        compiler_params=pltpu.CompilerParams(
            collective_id=0, has_side_effects=True, vmem_limit_bytes=48 * 1024 * 1024
        ),
    )(block_clip, queries[0], key_states[0], value_states[0], out_cotangent[0], out_weight)
    return out[None], dq[None], dk[None], dv[None], wg


def solution(mesh):
    tokens = P("dp", "ctx", None)
    return jax.shard_map(
        per_device,
        mesh=mesh,
        in_specs=(tokens, tokens, tokens, tokens, P(), P("dp", "ctx")),
        out_specs=(tokens, tokens, tokens, tokens, P("ctx", "dp")),
        check_vma=False,
    )
```

time: 424 us -> 103 us (0.24)
  waiting for transfers between devices: 246 us -> 0 us
  Pallas kernels: 0 us -> 90.9 us
  matrix products: 82.3 us -> 0 us
  starting transfers between devices: 28 us -> 0 us
  local copies, waits for them, and re-layouts: 30.1 us -> 9.01 us
  other arithmetic: 18.4 us -> 0 us
  between operations: 14.9 us -> 1.3 us
    unnamed x4 -> x0, waiting for transfers between devices: 194 us -> none
    pallas_call x0 -> x1, Pallas kernels: none -> 90.9 us  [per_device(): pl.pallas_call(kernel, out_shape=(shape((steps, dout), BF16), shape((step...]
    dot_general x66 -> x0, matrix products: 82.3 us -> none  [the longest x9 14.2 us: backward_one_group(): jnp.einsum('hqk,hqd->hkd', d_scores, query_head, preferred_element_type=j...]
    ppermute x10 -> x0, waiting for transfers between devices: 51.9 us -> none  [passed_along(): lax.ppermute(value, axis, [(source, source + steps) for source in range(f...]
    ppermute x10 -> x0, starting transfers between devices: 27.9 us -> none  [passed_along(): lax.ppermute(value, axis, [(source, source + steps) for source in range(f...]
    sub x9 -> x0, local copies, waits for them, and re-layouts: 6.2 us -> none  [backward_one_group(): probs = jnp.exp(scores - total_head[:, :, None])]
    unnamed x24 -> x15, local copies, waits for them, and re-layouts: 14.7 us -> 9.01 us
    dynamic_update_slice x9 -> x0, other arithmetic: 5.2 us -> none  [forward_block(): mixed, log_total = lax.map(forward_one_group, stacked)]
  transfers between devices with their start and end apart: 12 -> 0, of which waited for: 7 -> 0; matrix products, arithmetic and copies ran while one was open for 19% -> 0% of each run, Pallas kernels for 0% -> 0%
where the time goes in v1:
time: 103 us; the launch traced here: 101 us
  Pallas kernels  90.9 us (88%)
  local copies, waits for them, and re-layouts  9.01 us (9%)
  between operations  1.3 us (1%)
    pallas_call x1, Pallas kernels, per_device(): pl.pallas_call(kernel, out_shape=(shape((steps, dout), BF16), shape((step...  90.9 us
    unnamed x15, local copies, waits for them, and re-layouts  9.01 us

profile of v1, /device:TPU:6, one launch (start us, length us, event | category | flops | bytes accessed | tf_op | source)
XLA Modules:
  0.0 101.2 jit_solution(717175169176519909)
XLA Ops:
  1.3 0.0 copy-start
  1.3 1.7 %copy-done = bf16[1024,1152]{1,0:T(8,128)(2,1)S(1)} copy-done((bf16[1024,1152]{1,0:T(8,128)(2,1)S(1)}, bf16[1024,1152]{1,0:T(8,128)(2,1)}, u32[]{:S(2)}) %copy-start) | copy-done | bytes 2359320
  2.9 0.0 copy-start.1
  2.9 1.0 copy-done.1
  3.9 0.0 copy-start.2
  3.9 1.0 copy-done.2
  4.9 0.0 copy-start.3
  4.9 1.0 copy-done.3
  5.8 0.0 copy-start.4
  5.8 0.9 copy-done.4
  6.8 90.9 %shard_map.101 = (bf16[128,1024]{1,0:T(8,128)(2,1)S(1)}, bf16[128,1152]{1,0:T(8,128)(2,1)S(1)}, bf16[128,1152]{1,0:T(8,128)(2,1)S(1)}, bf16[128,1152]{1,0:T(8,128)(2,1)S(1)}, f32[64,24]{1,0:T(8,128)S(1)}) custom-call(s32[1,1]{1,0:T(1,128)S(6)} %copy.16.clip_ref, bf16[128,1152]{1,0:T(8,128)(2,1)S(1)} %bitcast.8, bf16[128,1152]{1,0:T(8,128)(2,1)S(1)} %bitcast.9, ...), custom_call_target="tpu_custom_call" | custom-call | tf_op jit(solution)/shard_map/pallas_call | solution.py:394
  97.7 0.7 copy.11
  98.4 0.7 copy.17
  99.1 0.7 copy.18
  99.8 0.7 copy.19
  100.5 0.7 copy.20
Async XLA Ops:
  1.3 1.7 %copy-start = (bf16[1024,1152]{1,0:T(8,128)(2,1)S(1)}, bf16[1024,1152]{1,0:T(8,128)(2,1)}, u32[]{:S(2)}) copy-start(bf16[1024,1152]{1,0:T(8,128)(2,1)} %w_ref.1) | copy-start | bytes 7077892
  2.9 1.0 copy-start.1
  3.9 1.0 copy-start.2
  4.9 1.0 copy-start.3
  5.8 0.9 copy-start.4

commit v2 on v1

v2 whole, which is shorter than its diff:
```python
import math

import jax
import jax.numpy as jnp
from jax import lax
from jax.experimental import pallas as pl
from jax.experimental.pallas import tpu as pltpu
from jax.sharding import PartitionSpec as P

HDIM = 64
BLOCK = 128
WIN = 256
GROUPS = 3
PAIR = 2 * HDIM
STAT = 32

NZ, NYH, NC = 12, 2, 2
NX, NYL = 4, 4

BF16 = jnp.bfloat16
F32 = jnp.float32
MESH = pl.DeviceIdType.MESH


def dot_nn(a, b):
    return lax.dot_general(a, b, (((1,), (0,)), ((), ())), preferred_element_type=F32)


def dot_nt(a, b):
    return lax.dot_general(a, b, (((1,), (1,)), ((), ())), preferred_element_type=F32)


def dot_tn(a, b):
    return lax.dot_general(a, b, (((0,), (0,)), ((), ())), preferred_element_type=F32)


def kernel(
    clip_ref, q_ref, k_ref, v_ref, cot_ref, w_ref,
    out_hbm, dq_hbm, dk_hbm, dv_hbm, wg_hbm,
    out_ref, dq_ref, dk_ref, dv_ref, wg_ref,
    q_buf, cot_buf, w_buf, kcat, vcat, clips, bias, da_buf, att_buf,
    own_k, own_v, qcat, dcat, next_clips, next_bias, stat_cols, stat_own, stat_in,
    g_buf, a_in, b_buf, b_in, y_out, y_in, z_src, z_in,
    in_sem, own_sem, res_sem, clip_sem, halo_sem, next_sem, stat_sem, a_sem, b_sem, z_send, z_recv, y_send, y_recv,
):
    dp, ctx = lax.axis_index("dp"), lax.axis_index("ctx")
    n_ctx = NX * NYL
    core = lax.rem(dp, NC)
    yh = lax.rem(dp // NC, NYH)
    z = dp // (NC * NYH)
    x, yl = ctx // NYL, lax.rem(ctx, NYL)
    here = yh * NYL + yl
    gw = q_ref.shape[1] // GROUPS
    dout = cot_ref.shape[1]
    dx = dout // NX
    zg = NZ // GROUPS
    rows = gw // (zg * NYH * NC)
    yw = dx // NYL
    yc = max(yw, 128)
    sharers = yc // yw
    zh = zg // sharers
    side = lax.rem(yl, sharers)

    right = (dp, lax.rem(ctx + 1, n_ctx))
    left = (dp, lax.rem(ctx + n_ctx - 1, n_ctx))
    sibling = (dp - core + (NC - 1 - core), ctx)

    def at_x(d):
        return (dp, lax.rem(x + d, NX) * NYL + yl)

    def at_z(zz, n):
        return ((zz * NYH + yh) * NC + core, ctx - side + n)

    def at_y(k):
        return ((z * NYH + k // NYL) * NC + core, x * NYL + lax.rem(k, NYL))

    stores = []

    def write(src, dst):
        copy = pltpu.make_async_copy(src, dst, res_sem.at[len(stores)])
        copy.start()
        stores.append(copy)

    loads = [
        pltpu.make_async_copy(src, dst, in_sem.at[n])
        for n, (src, dst) in enumerate(((cot_ref, cot_buf), (w_ref, w_buf), (q_ref, q_buf)))
    ]
    own_loads = [
        [
            pltpu.make_async_copy(
                src.at[:, pl.ds(g * gw, gw)], cat.at[g, pl.ds(2 * BLOCK, BLOCK), :], own_sem.at[g, n]
            )
            for n, (src, cat) in enumerate(((k_ref, kcat), (v_ref, vcat)))
        ]
        for g in range(GROUPS)
    ]
    for copy in loads:
        copy.start()
    for pair in own_loads:
        for copy in pair:
            copy.start()
    clips[2] = jnp.full((8, 128), clip_ref[0, 0], jnp.int32)
    next_clips[0] = jnp.full((8, 128), clip_ref[0, 0], jnp.int32)

    barrier = pltpu.get_barrier_semaphore()

    def hello(device):
        pl.semaphore_signal(barrier, inc=1, device_id=device, device_id_type=MESH)

    hello(right)
    hello(left)
    hello(sibling)
    for d in range(1, NX):
        hello(at_x(d))
    @pl.loop(0, NZ)
    def _(d):
        zz = lax.rem(z + d, NZ)
        for n in range(sharers):
            @pl.when((zz != z) | (side != n))
            def _():
                hello(at_z(zz, n))
    if NYH * NYL > 1:
        @pl.loop(1, NYH * NYL)
        def _(d):
            hello(at_y(lax.rem(here + d, NYH * NYL)))

    pl.semaphore_wait(barrier, 3 + (NX - 1) + (sharers * NZ - 1) + (NYH * NYL - 1))

    sends = []

    def remote(src, dst, send_sem, recv_sem, device):
        return pltpu.make_async_remote_copy(
            src_ref=src, dst_ref=dst, send_sem=send_sem, recv_sem=recv_sem,
            device_id=device, device_id_type=MESH,
        )

    def start(copy):
        copy.start()
        sends.append(copy)
        return copy

    def halo(g, hop):
        low = (1 - hop) * BLOCK
        part = []
        for number, (src, cat) in enumerate(((k_ref, kcat), (v_ref, vcat))):
            part.append(
                remote(
                    src.at[:, pl.ds(g * gw, gw)] if hop == 0 else cat.at[g, pl.ds(low + BLOCK, BLOCK), :],
                    cat.at[g, pl.ds(low, BLOCK), :],
                    halo_sem.at[0, hop, g, number],
                    halo_sem.at[1, hop, g, number],
                    right,
                )
            )
        return part

    def next_halo(g, hop):
        cols = pl.ds(g * gw, gw)
        return [
            remote(
                own.at[:, cols] if hop == 0 else cat.at[g, pl.ds(0, BLOCK), :],
                cat.at[g, pl.ds(hop * BLOCK, BLOCK), :],
                next_sem.at[0, hop, g, number],
                next_sem.at[1, hop, g, number],
                left,
            )
            for number, (own, cat) in enumerate(((q_ref, qcat), (da_buf, dcat)))
        ]

    def clip_hop(hop):
        return [
            remote(
                clips.at[2 - hop], clips.at[1 - hop],
                clip_sem.at[0, hop, 0], clip_sem.at[1, hop, 0], right,
            ),
            remote(
                next_clips.at[hop], next_clips.at[hop + 1],
                clip_sem.at[0, hop, 1], clip_sem.at[1, hop, 1], left,
            ),
        ]

    clip_hops = [clip_hop(0), clip_hop(1)]
    hops = [[halo(g, hop) for g in range(GROUPS)] for hop in range(2)]
    next_hops = [[next_halo(g, hop) for g in range(GROUPS)] for hop in range(2)]
    for copy in clip_hops[0]:
        start(copy)
    for g in range(GROUPS):
        for copy in hops[0][g]:
            start(copy)

    def d_attended(g):
        cols = slice(g * gw, (g + 1) * gw)
        da_buf[:, cols] = dot_nn(cot_buf[...], w_buf[:, cols]).astype(BF16)

    loads[0].wait()
    loads[1].wait()
    for n in range(2):
        clip_hops[0][n].wait_recv()
        start(clip_hops[1][n])
    for g in range(GROUPS):
        d_attended(g)
        for number in range(2):
            hops[0][g][number].wait_recv()
            start(hops[1][g][number])
        for copy in next_hops[0][g]:
            start(copy)
    for n in range(2):
        clip_hops[1][n].wait_recv()
    loads[2].wait()
    for pair in own_loads:
        for copy in pair:
            copy.wait()

    row = lax.broadcasted_iota(jnp.int32, (BLOCK, BLOCK), 0)
    col = lax.broadcasted_iota(jnp.int32, (BLOCK, BLOCK), 1)
    own_clip = clips[2, 0:1, :]
    for part in range(3):
        shown = clips[part, 0:1, :] == own_clip
        shown = jnp.broadcast_to(shown, (BLOCK, BLOCK))
        if part == 0:
            shown = shown & (col > row)
        if part == 2:
            shown = shown & (col <= row)
        shown = shown & (col + (ctx + part - 2) * BLOCK >= 0)
        term = jnp.where(shown, 0.0, -1e30).astype(F32)
        cols = slice(part * BLOCK, (part + 1) * BLOCK)
        bias[0:BLOCK, cols] = term
        bias[BLOCK:, cols] = term

    for part in range(2):
        shown = next_clips[part + 1, 0:1, :] == next_clips[0, 0:1, :]
        shown = jnp.broadcast_to(shown, (BLOCK, BLOCK))
        if part == 1:
            shown = shown & (row > col)
        shown = shown & (col * 0 + ctx + part + 1 < n_ctx)
        term = jnp.where(shown, 0.0, -1e30).astype(F32)
        cols = slice(part * BLOCK, (part + 1) * BLOCK)
        next_bias[0:BLOCK, cols] = term
        next_bias[BLOCK:, cols] = term

    stat_cols[...] = jnp.zeros_like(stat_cols)
    scaling = 1.0 / math.sqrt(HDIM)
    lane = lax.broadcasted_iota(jnp.int32, (BLOCK, PAIR), 1)
    low_head = lane < HDIM

    def stacked(value):
        return jnp.concatenate(
            [jnp.where(low_head, value, 0.0), jnp.where(low_head, 0.0, value)], axis=0
        )

    def picked(value):
        return jnp.where(low_head, value[:BLOCK], value[BLOCK:])

    def attention(g):
        @pl.loop(0, gw // PAIR)
        def _(p):
            lanes = pl.ds(pl.multiple_of(p * PAIR, PAIR), PAIR)
            whole = pl.ds(pl.multiple_of(g * gw + p * PAIR, PAIR), PAIR)
            q2 = stacked(q_buf[:, whole].astype(F32) * scaling).astype(BF16)
            da_f32 = stacked(da_buf[:, whole].astype(F32))
            da2 = da_f32.astype(BF16)
            keys = kcat[g, :, lanes]
            values = vcat[g, :, lanes]
            scores = dot_nt(q2, keys) + bias[...]
            top = jnp.max(scores, axis=1, keepdims=True)
            powers = jnp.exp(scores - top)
            total = jnp.sum(powers, axis=1, keepdims=True)
            probs = powers * (1.0 / total)
            weights = probs.astype(BF16)
            attended = picked(dot_nn(weights, values)).astype(BF16)
            att_buf[:, whole] = attended
            att_f32 = attended.astype(F32)
            delta = jnp.sum(da_f32 * jnp.concatenate([att_f32, att_f32], axis=0), axis=1, keepdims=True)
            log_total = top + jnp.log(total)
            d_weights = dot_nt(da2, values)
            d_scores = (probs * (d_weights - delta)).astype(BF16)
            dq_ref[:, whole] = (picked(dot_nn(d_scores, keys)) * scaling).astype(BF16)
            own_k[g, :, lanes] = dot_tn(d_scores[:, 2 * BLOCK :], q2)
            own_v[g, :, lanes] = dot_tn(weights[:, 2 * BLOCK :], da2)
            head = 2 * (g * (gw // PAIR) + p)
            stats = stat_cols[...]
            for n in range(2):
                part = slice(n * BLOCK, (n + 1) * BLOCK)
                stats = jnp.where(lane == head + n, log_total[part], stats)
                stats = jnp.where(lane == head + n + STAT, delta[part], stats)
            stat_cols[...] = stats

    def stat_copy(hop):
        return remote(
            stat_own if hop == 0 else stat_in.at[0], stat_in.at[hop],
            stat_sem.at[0, hop], stat_sem.at[1, hop], left,
        )

    stat_hops = [stat_copy(0), stat_copy(1)]

    def send_stats():
        stat_own[...] = stat_cols[...].T[: 2 * STAT]
        start(stat_hops[0])

    def relay(copies, later):
        for copy, after in zip(copies, later):
            copy.wait_recv()
            start(after)

    def key_side(g):
        for copy in next_hops[1][g]:
            copy.wait_recv()

        @pl.loop(0, gw // PAIR)
        def _(p):
            lanes = pl.ds(pl.multiple_of(p * PAIR, PAIR), PAIR)
            whole = pl.ds(pl.multiple_of(g * gw + p * PAIR, PAIR), PAIR)
            head = 2 * (g * (gw // PAIR) + p)

            def spread(offset):
                parts = []
                for n in range(2):
                    line = jnp.concatenate(
                        [stat_in[hop, pl.ds(head + n + offset, 1), :] for hop in range(2)], axis=1
                    )
                    parts.append(jnp.broadcast_to(line, (BLOCK, 2 * BLOCK)))
                return jnp.concatenate(parts, axis=0)

            k2 = stacked(kcat[g, 2 * BLOCK :, lanes].astype(F32) * scaling).astype(BF16)
            v2 = stacked(vcat[g, 2 * BLOCK :, lanes].astype(F32)).astype(BF16)
            next_q = qcat[g, :, lanes]
            next_d = dcat[g, :, lanes]
            probs = jnp.exp(dot_nt(k2, next_q) + next_bias[...] - spread(0))
            weights = probs.astype(BF16)
            d_scores = (probs * (dot_nt(v2, next_d) - spread(STAT))).astype(BF16)
            key_part = picked(dot_nn(d_scores, next_q)) * scaling
            value_part = picked(dot_nn(weights, next_d))
            dk_ref[:, whole] = (own_k[g, :, lanes] + key_part).astype(BF16)
            dv_ref[:, whole] = (own_v[g, :, lanes] + value_part).astype(BF16)

        cols = pl.ds(g * gw, gw)
        write(dk_ref.at[:, cols], dk_hbm.at[:, cols])
        write(dv_ref.at[:, cols], dv_hbm.at[:, cols])

    half = gw // NC

    def a_copy(g):
        return remote(
            g_buf.at[NC - 1 - core, g], a_in.at[g], a_sem.at[0, g], a_sem.at[1, g], sibling
        )

    a_copies = [a_copy(g) for g in range(GROUPS)]

    def weight_terms(g):
        for part in range(NX):
            terms = dot_tn(
                att_buf[:, g * gw : (g + 1) * gw], cot_buf[:, part * dx : (part + 1) * dx]
            ).reshape(zg * NYH, NC, rows, dx)
            for number in range(NC):
                g_buf[number, g, part] = terms[:, number].reshape(half, dx).astype(BF16)
        start(a_copies[g])

    def b_copy(g, d):
        return remote(
            b_buf.at[g, lax.rem(x + d, NX)], b_in.at[g, d - 1],
            b_sem.at[0, g, d - 1], b_sem.at[1, g, d - 1], at_x(d),
        )

    b_copies = [[b_copy(g, d) for d in range(1, NX)] for g in range(GROUPS)]

    def after_core(g):
        a_copies[g].wait_recv()
        for part in range(NX):
            b_buf[g, part] = (g_buf[core, g, part].astype(F32) + a_in[g, part].astype(F32)).astype(BF16)
        for copy in b_copies[g]:
            start(copy)

    def y_copy(g, k):
        return remote(y_out.at[g, k], y_in.at[g, here], y_send.at[g, k], y_recv.at[g, here], at_y(k))

    def y_arrival(g, s):
        return remote(y_out.at[g, s], y_in.at[g, s], y_send.at[g, s], y_recv.at[g, s], at_y(s))

    def after_x(g):
        total = b_buf[g, x].astype(F32)
        for d in range(1, NX):
            b_copies[g][d - 1].wait_recv()
            total = total + b_in[g, d - 1].astype(F32)
        total = total.reshape(zg, NYH, rows, dx)
        for k in range(NYH * NYL):
            high, low = (k % NYL) // sharers, k % sharers
            piece = total[low * zh : (low + 1) * zh, k // NYL, :, high * yc : (high + 1) * yc]
            y_out[g, k] = piece.reshape(zh * rows, yc).astype(BF16)

            @pl.when(k != here)
            def _():
                y_copy(g, k).start()

            @pl.when(k == here)
            def _():
                y_in[g, here] = y_out[g, k]

    def z_copy(g, j, n):
        zz = g * zg + side * zh + j
        return remote(z_src.at[g, j], z_in.at[z], z_send.at[g, j, n], z_recv.at[z], at_z(zz, n))

    def after_y(g):
        @pl.loop(0, NYH * NYL)
        def _(s):
            @pl.when(s != here)
            def _():
                y_arrival(g, s).wait_recv()

        total = y_in[g, 0].astype(F32)
        for s in range(1, NYH * NYL):
            total = total + y_in[g, s].astype(F32)
        for j in range(zh):
            z_src[g, j] = total[j * rows : (j + 1) * rows]
            for n in range(sharers):
                mine = (g * zg + side * zh + j == z) & (side == n)

                @pl.when(jnp.logical_not(mine))
                def _():
                    z_copy(g, j, n).start()

                @pl.when(mine)
                def _():
                    z_in[z] = z_src[g, j]

    def after_z():
        source_side = lax.rem(z, zg) // zh

        @pl.loop(0, NZ)
        def _(s):
            @pl.when((s != z) | (source_side != side))
            def _():
                remote(
                    z_src.at[0, 0], z_in.at[s], z_send.at[0, 0, 0], z_recv.at[s], at_z(s, source_side)
                ).wait_recv()
        total = z_in[0]
        for s in range(1, NZ):
            total = total + z_in[s]
        mine = total[:, 0:yw]
        for n in range(1, sharers):
            mine = jnp.where(side == n, total[:, n * yw : (n + 1) * yw], mine)
        wg_ref[...] = mine
        write(wg_ref, wg_hbm)

    def project(part):
        piece = slice(part * dx, (part + 1) * dx)
        out_ref[:, piece] = dot_nt(att_buf[...], w_buf[piece, :]).astype(BF16)

    for g in range(GROUPS):
        for copy in hops[1][g]:
            copy.wait_recv()
        attention(g)
        cols = pl.ds(g * gw, gw)
        write(dq_ref.at[:, cols], dq_hbm.at[:, cols])
        if g >= 1:
            relay(next_hops[0][g - 1], next_hops[1][g - 1])
        weight_terms(g)
        if g >= 1:
            after_core(g - 1)
        if g >= 2:
            after_x(g - 2)
    send_stats()
    after_core(GROUPS - 1)
    relay(next_hops[0][GROUPS - 1], next_hops[1][GROUPS - 1])
    after_x(1)
    after_y(0)
    relay(stat_hops[:1], stat_hops[1:])
    after_x(2)
    for part in range(NX):
        project(part)
    write(out_ref, out_hbm)
    after_y(1)
    after_y(2)
    stat_hops[1].wait_recv()
    key_side(0)
    after_z()
    key_side(1)
    key_side(2)

    for copy in stores:
        copy.wait()
    for copy in sends:
        copy.wait_send()

    for g in range(GROUPS):
        @pl.loop(0, NYH * NYL)
        def _(s):
            @pl.when(s != here)
            def _():
                y_arrival(g, s).wait_send()

        for j in range(zh):
            for n in range(sharers):
                @pl.when((g * zg + side * zh + j != z) | (side != n))
                def _():
                    z_copy(g, j, n).wait_send()


def store(*refs):
    sources, results, held, sem = refs[:5], refs[5:10], refs[10:15], refs[15]
    loads = [pltpu.make_async_copy(sources[n], held[n], sem.at[0, n]) for n in range(5)]
    stores = [pltpu.make_async_copy(held[n], results[n], sem.at[1, n]) for n in range(5)]
    for copy in loads:
        copy.start()
    for load, copy in zip(loads, stores):
        load.wait()
        copy.start()
    for copy in stores:
        copy.wait()


def per_device(queries, key_states, value_states, out_cotangent, out_weight, block_clip):
    steps, width = queries.shape[1:]
    dout = out_cotangent.shape[2]
    gw = width // GROUPS
    dx = dout // NX
    zg = NZ // GROUPS
    rows = gw // (zg * NYH * NC)
    half = gw // NC
    yw = dx // NYL
    yc = max(yw, 128)
    ny = NYH * NYL
    zh = zg * yw // yc
    shape = jax.ShapeDtypeStruct
    vmem = pltpu.VMEM
    dma = pltpu.SemaphoreType.DMA
    group_f32 = vmem((GROUPS, BLOCK, gw), F32)
    out, dq, dk, dv, wg = pl.pallas_call(
        kernel,
        out_shape=(
            shape((steps, dout), BF16),
            shape((steps, width), BF16),
            shape((steps, width), BF16),
            shape((steps, width), BF16),
            shape((rows, yw), F32),
        ),
        in_specs=[pl.BlockSpec(memory_space=pltpu.SMEM)] + [pl.BlockSpec(memory_space=pltpu.HBM)] * 5,
        out_specs=tuple([pl.BlockSpec(memory_space=pltpu.HBM)] * 5),
        scratch_shapes=[
            vmem((steps, dout), BF16),
            vmem((steps, width), BF16),
            vmem((steps, width), BF16),
            vmem((steps, width), BF16),
            vmem((rows, yw), F32),
            vmem((steps, width), BF16),
            vmem((steps, dout), BF16),
            vmem((dout, width), BF16),
            vmem((GROUPS, WIN + BLOCK, gw), BF16),
            vmem((GROUPS, WIN + BLOCK, gw), BF16),
            vmem((3, 8, 128), jnp.int32),
            vmem((2 * BLOCK, WIN + BLOCK), F32),
            vmem((steps, width), BF16),
            vmem((steps, width), BF16),
            group_f32,
            group_f32,
            vmem((GROUPS, WIN, gw), BF16),
            vmem((GROUPS, WIN, gw), BF16),
            vmem((3, 8, 128), jnp.int32),
            vmem((2 * BLOCK, WIN), F32),
            vmem((BLOCK, BLOCK), F32),
            vmem((2 * STAT, BLOCK), F32),
            vmem((2, 2 * STAT, BLOCK), F32),
            vmem((NC, GROUPS, NX, half, dx), BF16),
            vmem((GROUPS, NX, half, dx), BF16),
            vmem((GROUPS, NX, half, dx), BF16),
            vmem((GROUPS, max(NX - 1, 1), half, dx), BF16),
            vmem((GROUPS, ny, zh * rows, yc), BF16),
            vmem((GROUPS, ny, zh * rows, yc), BF16),
            vmem((GROUPS, zh, rows, yc), F32),
            vmem((NZ, rows, yc), F32),
            dma((3,)),
            dma((GROUPS, 2)),
            dma((3 * GROUPS + 2,)),
            dma((2, 2, 2)),
            dma((2, 2, GROUPS, 2)),
            dma((2, 2, GROUPS, 2)),
            dma((2, 2)),
            dma((2, GROUPS)),
            dma((2, GROUPS, max(NX - 1, 1))),
            dma((GROUPS, zh, yc // yw)),
            dma((NZ,)),
            dma((GROUPS, ny)),
            dma((GROUPS, ny)),
        ],
        compiler_params=pltpu.CompilerParams(
            collective_id=0, has_side_effects=True, vmem_limit_bytes=60 * 1024 * 1024
        ),
    )(block_clip, queries[0], key_states[0], value_states[0], out_cotangent[0], out_weight)
    results = (out, dq, dk, dv, wg)
    out, dq, dk, dv, wg = pl.pallas_call(
        store,
        out_shape=tuple(shape(r.shape, r.dtype) for r in results),
        in_specs=[pl.BlockSpec(memory_space=pl.ANY)] * 5,
        out_specs=tuple([pl.BlockSpec(memory_space=pltpu.HBM)] * 5),
        scratch_shapes=[vmem(r.shape, r.dtype) for r in results] + [dma((2, 5))],
        compiler_params=pltpu.CompilerParams(vmem_limit_bytes=60 * 1024 * 1024),
    )(*results)
    return out[None], dq[None], dk[None], dv[None], wg.T


def solution(mesh):
    tokens = P("dp", "ctx", None)
    return jax.shard_map(
        per_device,
        mesh=mesh,
        in_specs=(tokens, tokens, tokens, tokens, P(), P("dp", "ctx")),
        out_specs=(tokens, tokens, tokens, tokens, P("ctx", "dp")),
        check_vma=False,
    )
```

time: 103 us -> 95.4 us (0.926)
  local copies, waits for them, and re-layouts: 9.01 us -> 0 us
  Pallas kernels: 90.9 us -> 92.9 us
    unnamed x15 -> x0, local copies, waits for them, and re-layouts: 9.01 us -> none
    pallas_call x0 -> x1, Pallas kernels: none -> 2.04 us  [per_device(): pl.pallas_call(store, out_shape=tuple((shape(r.shape, r.dtype) for r in r...]
where the time goes in v2:
time: 95.4 us; the launch traced here: 94.2 us
  Pallas kernels  92.9 us (97%)
  between operations  1.29 us (1%)
    pallas_call x1, Pallas kernels, per_device(): pl.pallas_call(kernel, out_shape=(shape((steps, dout), BF16), shape((step...  90.8 us
    pallas_call x1, Pallas kernels, per_device(): pl.pallas_call(store, out_shape=tuple((shape(r.shape, r.dtype) for r in r...  2.04 us

profile of v2, /device:TPU:6, one launch (start us, length us, event | category | flops | bytes accessed | tf_op | source)
XLA Modules:
  0.0 94.2 jit_solution(15080234145120835500)
XLA Ops:
  1.3 90.8 %shard_map.101 = (bf16[128,1024]{1,0:T(8,128)(2,1)}, bf16[128,1152]{1,0:T(8,128)(2,1)}, bf16[128,1152]{1,0:T(8,128)(2,1)}, bf16[128,1152]{1,0:T(8,128)(2,1)}, f32[24,64]{1,0:T(8,128)}) custom-call(s32[1,1]{1,0:T(1,128)S(6)} %copy.11.clip_ref, bf16[128,1152]{1,0:T(8,128)(2,1)} %bitcast.9, bf16[128,1152]{1,0:T(8,128)(2,1)} %bitcast.10, ...), custom_call_target="tpu_custom_call" | custom-call | tf_op jit(solution)/shard_map/pallas_call | solution.py:527
  92.1 2.0 %shard_map.102 = (bf16[128,1024]{1,0:T(8,128)(2,1)}, bf16[128,1152]{1,0:T(8,128)(2,1)}, bf16[128,1152]{1,0:T(8,128)(2,1)}, bf16[128,1152]{1,0:T(8,128)(2,1)}, f32[24,64]{1,0:T(8,128)}) custom-call(bf16[128,1024]{1,0:T(8,128)(2,1)} %get-tuple-element.15.refs_0_, bf16[128,1152]{1,0:T(8,128)(2,1)} %get-tuple-element.16.refs_1_, ...), custom_call_target="tpu_custom_call" | custom-call | tf_op jit(solution)/shard_map/pallas_call | solution.py:589
